TPU v7x, 32 devices: a whole 2x2x4 slice. The times are simulated.
32 devices in a mesh: dp: 4 (over y, core), ctx: 8 (over z, x).
Axes of the slice: x: 2, y: 2, z: 4, core: 2. Of those that a mesh axis runs over, the one named last changes fastest.
Arguments:
- features: bfloat16 [4, 8, 248, 12288], P('dp', 'ctx'), may hold values from -6 to 6
- counts: int32 [4, 8], P('dp', 'ctx'), may hold values from 8 to 248, as said below
- short_taps: float32 [7, 3, 4096], P(None, None, 'ctx'), may hold values from -2 to 2
- residue: float32 [16, 256], P(None, 'ctx'), may hold values from -0.25 to 0.25
- decay_rate: float32 [16, 256], P(None, 'ctx'), may hold values from 1.953125e-05 to 0.05
- skip_gain: float32 [4096], P('ctx'), may hold values from -4 to 4
- cotangent: bfloat16 [4, 8, 248, 4096], P('dp', 'ctx'), may hold values from -6 to 6
Outputs:
- output: bfloat16 [4, 8, 248, 4096], P('dp', 'ctx')
- grad_features: bfloat16 [4, 8, 248, 12288], P('dp', 'ctx')
- grad_taps: float32 [7, 3, 4096], P(None, None, 'ctx')
- grad_residue: float32 [16, 256], P(None, 'ctx')
- grad_skip: float32 [4096], P('ctx')
Inputs may be any that keep to these rules, and one draw needn't show every extreme that they name: Along ctx the loader shards come in pairs 2m, 2m + 1 whose counts sum to 256; each replica has a shard holding exactly 248 rows; the counts of a replica sum to 1024.
All inputs are finite; a program needn't handle non-finite values.
Results may differ from a plain program's by a relative error of at most 0.0069.
Values may be sent and summed in bfloat16 or wider, within the bound.
A program may use at most 128 MiB of HBM per device.

v0:
```python
import jax
import jax.numpy as jnp
from jax import lax
from jax.sharding import PartitionSpec as P

TAPS = 7
TOK_DEV = 128


def modal_local(mixed, d_long, residue, decay_rate, row_block):
    highest = lax.Precision.HIGHEST
    length, channels = mixed.shape
    groups = residue.shape[1]
    group_size = channels // groups
    block_count = length // row_block
    lag_steps = jnp.arange(row_block, dtype=jnp.float32)
    decay_col = decay_rate[:, :, None]
    lag_powers = jnp.exp(-decay_col * lag_steps)
    kernel_rows = jnp.sum(residue[:, :, None] * lag_powers, axis=0)
    lag_int = jnp.arange(row_block, dtype=jnp.int32)
    lag_grid = lag_int[:, None] - lag_int[None, :]
    lower_part = lag_grid >= 0
    toeplitz = jnp.where(
        lower_part[None], jnp.take(kernel_rows, jnp.clip(lag_grid, 0, row_block - 1), axis=1), 0.0
    )
    out_powers = jnp.exp(-decay_col * (lag_steps + 1.0))
    in_powers = jnp.exp(-decay_col * (row_block - 1.0 - lag_steps))
    res_out = residue[:, :, None] * out_powers
    block_ids = jnp.arange(block_count, dtype=jnp.float32)
    block_gap = block_ids[:, None] - 1.0 - block_ids[None, :]
    carry_decay = jnp.where(
        block_gap >= 0.0,
        jnp.exp(-decay_rate[:, :, None, None] * row_block * jnp.maximum(block_gap, 0.0)),
        0.0,
    )
    lag_float = jnp.maximum(lag_grid, 0).astype(jnp.float32)
    mixed_blocks = mixed.reshape(block_count, row_block, groups, group_size)
    grad_blocks = d_long.reshape(block_count, row_block, groups, group_size)
    intra = jnp.einsum("gab,nbgq->nagq", toeplitz, mixed_blocks, precision=highest)
    local_state = jnp.einsum("rgb,nbgq->nrgq", in_powers, mixed_blocks, precision=highest)
    cross_state = jnp.einsum("rgij,jrgq->irgq", carry_decay, local_state, precision=highest)
    cross = jnp.einsum("rga,irgq->iagq", res_out, cross_state, precision=highest)
    long_part = (intra + cross).reshape(length, channels)
    du_intra = jnp.einsum("gab,nagq->nbgq", toeplitz, grad_blocks, precision=highest)
    d_cross = jnp.einsum("rga,iagq->irgq", res_out, grad_blocks, precision=highest)
    d_local = jnp.einsum("rgij,irgq->jrgq", carry_decay, d_cross, precision=highest)
    du_cross = jnp.einsum("rgb,nrgq->nbgq", in_powers, d_local, precision=highest)
    mixed_part = (du_intra + du_cross).reshape(length, channels)
    pair_sums = jnp.einsum("nagq,nbgq->gab", grad_blocks, mixed_blocks, precision=highest)

    def one_pole(pole_rates):
        weight = jnp.where(
            lower_part[None], jnp.exp(-pole_rates[:, None, None] * lag_float[None]), 0.0
        )
        return jnp.sum(pair_sums * weight, axis=(1, 2))

    grad_res = lax.map(one_pole, decay_rate)
    grad_res = grad_res + jnp.einsum(
        "iagq,rga,irgq->rg", grad_blocks, out_powers, cross_state, precision=highest
    )
    return (long_part, mixed_part, grad_res)


def moved_operator(features, counts, short_taps, residue, decay_rate, skip_gain, cotangent):
    shards = lax.axis_size("ctx")
    capacity = features.shape[2]
    model_width = cotangent.shape[3]
    channels = short_taps.shape[2]
    window_len = TOK_DEV * shards
    loader_in = features[0, 0].reshape(capacity, 3, model_width)
    cot_rows = cotangent[0, 0].reshape(capacity, 1, model_width)
    slot_ids = jnp.arange(capacity, dtype=jnp.int32)
    all_counts = lax.all_gather(counts, "ctx", axis=1, tiled=True)[0]
    shard_ends = jnp.cumsum(all_counts)
    shard_starts = shard_ends - all_counts
    positions = jnp.arange(window_len, dtype=jnp.int32)
    passed = shard_ends[None, :] <= positions[:, None]
    shard_of = jnp.sum(passed.astype(jnp.int32), axis=1)
    before = jnp.sum(jnp.where(passed, all_counts[None, :], 0), axis=1)
    take_index = shard_of * capacity + positions - before
    back_index = jnp.clip(shard_starts[:, None] + slot_ids[None, :], 0, window_len - 1).reshape(-1)
    back_valid = (slot_ids[None, :] < all_counts[:, None]).reshape(-1)

    def place(received):
        return jnp.take(received, take_index, axis=0)

    def inbound(loader_rows):
        return place(lax.all_to_all(loader_rows, "ctx", split_axis=2, concat_axis=0, tiled=True))

    def outbound(chan_rows):
        picked = jnp.take(chan_rows, back_index, axis=0)
        picked = jnp.where(back_valid[:, None, None], picked, jnp.zeros_like(picked))
        return lax.all_to_all(picked, "ctx", split_axis=0, concat_axis=2, tiled=True)

    window = inbound(loader_in)
    grad_chan = inbound(cot_rows)[:, 0, :]
    padded = jnp.pad(window, ((TAPS - 1, 0), (0, 0), (0, 0)))
    short_out = jnp.zeros((window_len, 3, channels), jnp.float32)
    for tap_index in range(TAPS):
        piece = padded[TAPS - 1 - tap_index : TAPS - 1 - tap_index + window_len].astype(jnp.float32)
        short_out = short_out + short_taps[tap_index] * piece
    short_b = short_out.astype(jnp.bfloat16)
    query_f = short_b[:, 0].astype(jnp.float32)
    key_f = short_b[:, 1].astype(jnp.float32)
    value_f = short_b[:, 2].astype(jnp.float32)
    mixed = (key_f * value_f).astype(jnp.bfloat16).astype(jnp.float32)
    grad_f = grad_chan.astype(jnp.float32)
    d_long = grad_f * query_f
    long_part, mixed_part, grad_res = modal_local(mixed, d_long, residue, decay_rate, 128)
    long_out = long_part + skip_gain * mixed
    gated = (query_f * long_out).astype(jnp.bfloat16)
    gated_rows = outbound(gated[:, None, :])
    d_query = grad_f * long_out
    d_mixed = mixed_part + skip_gain * d_long
    grad_gain = jnp.sum(d_long * mixed, axis=0)
    d_short = jnp.stack([d_query, d_mixed * value_f, d_mixed * key_f], axis=1)
    tail = jnp.pad(d_short, ((0, TAPS - 1), (0, 0), (0, 0)))
    d_window = jnp.zeros((window_len, 3, channels), jnp.float32)
    tap_grads = []
    for tap_index in range(TAPS):
        d_window = d_window + short_taps[tap_index] * tail[tap_index : tap_index + window_len]
        piece = padded[TAPS - 1 - tap_index : TAPS - 1 - tap_index + window_len].astype(jnp.float32)
        tap_grads.append(jnp.sum(d_short * piece, axis=0))
    grad_rows = outbound(d_window.astype(jnp.bfloat16))
    return (
        gated_rows.reshape(1, 1, capacity, model_width),
        grad_rows.reshape(1, 1, capacity, 3 * model_width),
        jnp.stack(tap_grads, axis=0),
        grad_res,
        grad_gain,
    )


def per_device(features, counts, short_taps, residue, decay_rate, skip_gain, cotangent):
    results = moved_operator(
        features, counts, short_taps, residue, decay_rate, skip_gain, cotangent
    )
    grad_tap, grad_res, grad_gain = lax.psum((results[2], results[3], results[4]), "dp")
    return (results[0], results[1], grad_tap, grad_res, grad_gain)


def solution(mesh):
    in_specs = (
        P("dp", "ctx", None, None),
        P("dp", "ctx"),
        P(None, None, "ctx"),
        P(None, "ctx"),
        P(None, "ctx"),
        P("ctx"),
        P("dp", "ctx", None, None),
    )
    out_specs = (
        P("dp", "ctx", None, None),
        P("dp", "ctx", None, None),
        P(None, None, "ctx"),
        P(None, "ctx"),
        P("ctx"),
    )
    return jax.shard_map(
        per_device, mesh=mesh, in_specs=in_specs, out_specs=out_specs, check_vma=False
    )
```

profile of v0, /device:TPU:0, one launch (start us, length us, event | category | flops | bytes accessed | tf_op | source)
XLA Modules:
  0.0 809.5 jit_solution(16444914577203407402)
XLA Ops:
  0.6 10.0 %copy.211 = bf16[248,1,4096]{0,1,2:T(2,128)(2,1)} copy(bf16[248,1,4096]{2,0,1:T(8,128)(2,1)} %bitcast.210) | data formatting | bytes 4063232 | tf_op jit(solution)/shard_map/reshape;squeeze | solution.py:71
  11.1 23.6 %reduce.2 = bf16[4096,248]{1,0:T(8,128)(2,1)S(1)} reduce(bf16[4096,1,248]{2,1,0:T(2,128)(2,1)} %bitcast.196, bf16[]{:T(256)} %broadcast.388), dimensions={1}, to_apply=%bitcast.179.reduce_sub_computation | reduce | bytes 4063234
  34.7 6.0 reshape.459
  40.8 7.3 all-to-all-start.2
  48.0 8.4 %copy.192 = bf16[1,1,248,12288]{2,3,1,0:T(8,128)(2,1)} copy(bf16[1,1,248,12288]{3,2,1,0:T(8,128)(2,1)} %param.9) | data formatting | bytes 12189696 | tf_op args[0]
  56.5 10.4 %copy.193 = bf16[248,3,4096]{0,1,2:T(4,128)(2,1)} copy(bf16[248,3,4096]{0,2,1:T(8,128)(2,1)} %bitcast.192) | data formatting | bytes 12189696 | tf_op jit(solution)/shard_map/reshape;squeeze | solution.py:70
  66.9 27.9 %all-to-all-done.2 = bf16[8,2,63488]{2,1,0:T(2,128)(2,1)S(1)} async-done(((bf16[8,2,63488]{2,1,0:T(2,128)(2,1)}), bf16[8,2,63488]{2,1,0:T(2,128)(2,1)S(1)}, u32[]{:S(2)}, u32[]{:S(2)}) %all-to-all-start.2) | async-done | bytes 2031648 | tf_op jit(solution)/shard_map/all_to_all | solution.py:88
  94.9 5.0 all-to-all-start
  101.8 180.5 %all-reduce.2 = s32[8]{0:T(128)S(1)} all-reduce(s32[8]{0:T(128)S(1)} %bitcast_dynamic-update-slice_fusion), channel_id=1, replica_groups=mesh['dp'=4,'ctx'=8] {'ctx'}, use_global_device_ids=true, to_apply=%add.2 | all-reduce | flops 8 | bytes 64 | tf_op jit(solution)/shard_map/lt | solution.py:82
  283.5 54.4 %gather_fusion.1 = f32[16384,32]{1,0:T(8,128)} fusion(f32[32,128]{0,1:T(8,128)S(1)} %copy.201, s32[16384]{0:T(1024)S(1)} %fusion.91), kind=kCustom, calls=%fused_computation.1 | custom fusion | bytes 4259840 | tf_op jit(solution)/shard_map/jit(_take)/gather | solution.py:24
  337.9 6.5 copy.202
  344.9 8.7 %reshape.460 = bf16[4096,1,248]{2,1,0:T(2,128)(2,1)} reshape(bf16[8,2,63488]{2,1,0:T(2,128)(2,1)S(1)} %all-to-all-done.2) | data formatting | bytes 4063232
  360.9 4.0 gather_fusion.3
  366.6 13.0 %copy.239 = bf16[248,3,8,512]{3,0,2,1:T(8,128)(2,1)} copy(bf16[248,3,8,512]{0,1,3,2:T(4,128)(2,1)} %bitcast.6) | data formatting | bytes 12189696 | tf_op jit(solution)/shard_map/all_to_all | solution.py:88
  379.6 23.3 %copy.196 = bf16[1984,3,512]{2,1,0:T(4,128)(2,1)} copy(bf16[1984,3,512]{2,0,1:T(8,128)(2,1)} %bitcast.193) | data formatting | bytes 12189696 | tf_op jit(solution)/shard_map/all_to_all | solution.py:88
  402.9 14.0 %gather_fusion = bf16[1024,3,512]{2,1,0:T(4,128)(2,1)} fusion(bf16[1984,3,512]{2,1,0:T(4,128)(2,1)} %copy.196, s32[1024]{0:T(1024)S(1)} %broadcast_clamp_fusion), kind=kCustom, calls=%fused_computation | custom fusion | bytes 6295552 | tf_op jit(solution)/shard_map/jit(_take)/gather | solution.py:85
  416.9 3.1 copy_select_fusion
  420.0 5.8 fusion.11
  433.0 3.9 copy.204
  441.2 4.8 fusion.35
  446.0 4.4 fusion.32
  450.7 3.9 fusion.45
  454.7 3.8 fusion.26
  465.8 2.9 copy.208
  468.8 3.8 copy.218
  472.6 5.7 fusion.42
  478.3 4.4 add_bitcast_fusion
  487.7 2.9 copy.221
  490.6 6.1 convert_multiply_fusion.15
  496.8 9.2 %gather_fusion.2 = bf16[1984,512]{1,0:T(8,128)(2,1)} fusion(bf16[1024,512]{1,0:T(8,128)(2,1)S(1)} %get-tuple-element.108, s32[2048]{0:T(1024)S(1)} %pad_clamp_fusion), kind=kCustom, calls=%fused_computation.2 | custom fusion | bytes 4071168 | tf_op jit(solution)/shard_map/jit(_take)/gather | solution.py:91
  506.0 3.8 fusion.36
  509.7 4.4 reduce.3
  514.2 5.9 reshape.457
  520.1 4.3 all-to-all-start.1
  524.4 13.9 %fusion.18 = (f32[3,512]{1,0:T(4,128)S(1)}, f32[3,512]{1,0:T(4,128)S(1)}, f32[3,512]{1,0:T(4,128)S(1)}, f32[3,512]{1,0:T(4,128)S(1)}, f32[3,512]{1,0:T(4,128)S(1...) fusion(bf16[1024,3,512]{2,0,1:T(8,128)(2,1)} %copy-done.3, ...), kind=kLoop, calls=%fused_computation.40 | loop fusion | flops 36165120 | bytes 15771648 | tf_op jit(solution)/shard_map/reduce_sum | solution.py:123
  538.3 5.2 add_convert_fusion
  543.6 4.7 copy.222
  548.3 23.6 %gather_fusion.4 = bf16[1984,3,512]{2,1,0:T(4,128)(2,1)} fusion(bf16[1024,3,512]{2,1,0:T(4,128)(2,1)} %copy.222, s32[2048]{0:T(1024)S(1)} %pad_clamp_fusion), kind=kCustom, calls=%fused_computation.4 | custom fusion | bytes 12197632 | tf_op jit(solution)/shard_map/jit(_take)/gather | solution.py:91
  571.9 16.4 %fusion.25 = f32[16,32]{0,1:T(8,128)S(1)} fusion(f32[16,32,8,16]{3,2,1,0:T(8,128)} %bitcast.195, f32[8,128,32,16]{1,0,3,2:T(8,128)S(1)} %convert_multiply_fusion.20, f32[128]{0:T(128)S(1)} %iota_add_fusion, f32[16,32]{0,1:T(8,128)S(1)} %copy.200), kind=kOutput, calls=%fused_computation.59 | convolution fusion | flops 100859392 | bytes 2363904 | tf_op jit(solution)/shard_map/iagq,rga,irgq->rg/dot_general | solution.py:58
  588.3 3.8 convolution_bitcast_fusion
  592.6 11.9 %select_select_fusion = bf16[1984,3,512]{2,1,0:T(4,128)(2,1)} fusion(bf16[1984,3,512]{2,1,0:T(4,128)(2,1)S(1)} %copy-done.2, pred[1984]{0:T(1024)(128)(4,1)S(1)} %compare_and_fusion, pred[1984]{0:T(1024)(128)(4,1)S(1)} %lt.99), kind=kLoop, calls=%fused_computation.12 | loop fusion | flops 6094848 | bytes 12193664 | tf_op jit(solution)/shard_map/jit(_where)/select_n | solution.py:92
  604.5 5.9 all-to-all-start.3
  610.4 11.9 %while.11 = (s32[]{:T(128)}, f32[16,32]{1,0:T(8,128)S(1)}, f32[16,32]{1,0:T(8,128)S(1)}, f32[32,128,128]{2,1,0:T(8,128)S(1)}, s32[]{:T(128)}, /*index=5*/s32[]{:T(128)}) while((s32[]{:T(128)}, f32[16,32]{1,0:T(8,128)S(1)}, f32[16,32]{1,0:T(8,128)S(1)}, f32[32,128,128]{2,1,0:T(8,128)S(1)}, s32[]{:T(128)}, ...), condition=%wide.region_14.15_spmd.clone, body=%wide.region_12.14_spmd.clone.sunk | while | flops 2179074 | bytes 2261845 | solution.py:57
  622.4 12.4 %all-reduce.3 = (f32[7,3,512]{2,1,0:T(4,128)S(1)}, f32[16,32]{1,0:T(8,128)}, f32[512]{0:T(512)}) all-reduce(f32[7,3,512]{2,1,0:T(4,128)S(1)} %constant_dynamic-update-slice_fusion, f32[16,32]{1,0:T(8,128)S(1)} %add.246, f32[512]{0:T(512)S(1)} %get-tuple-element.99), channel_id=1, replica_groups=mesh['dp'=4,'ctx'=8] {'dp'}, use_global_device_ids=true, to_apply=%region_11.12 | all-reduce | flops 11776 | bytes 94208 | tf_op jit(solution)/shard_map/psum | solution.py:138
  635.5 6.8 reshape.458
  647.9 139.1 %all-to-all-done.3 = bf16[1984,3,512]{2,1,0:T(4,128)(2,1)} async-done(((bf16[1984,3,512]{2,1,0:T(4,128)(2,1)}), bf16[1984,3,512]{2,1,0:T(4,128)(2,1)}, u32[]{:S(2)}, u32[]{:S(2)}) %all-to-all-start.3) | async-done | bytes 6094880 | tf_op jit(solution)/shard_map/all_to_all | solution.py:93
  787.0 12.5 %copy.223 = bf16[248,3,8,512]{3,2,1,0:T(8,128)(2,1)} copy(bf16[248,3,8,512]{3,1,0,2:T(4,128)(2,1)} %bitcast.43) | data formatting | bytes 12189696 | tf_op jit(solution)/shard_map/all_to_all | solution.py:93
  799.5 9.8 %reshape.389 = bf16[1,1,248,12288]{3,2,1,0:T(8,128)(2,1)} reshape(bf16[248,3,8,512]{3,2,1,0:T(8,128)(2,1)} %copy.223) | data formatting | bytes 12189696 | tf_op jit(solution)/shard_map/reshape | solution.py:127
  (185 shorter events, 54.6 us)
Async XLA Ops:
  40.8 54.1 %all-to-all-start.2 = ((bf16[8,2,63488]{2,1,0:T(2,128)(2,1)}), bf16[8,2,63488]{2,1,0:T(2,128)(2,1)S(1)}, u32[]{:S(2)}, u32[]{:S(2)}) async-start(bf16[8,2,63488]{2,1,0:T(2,128)(2,1)} %reshape.459), calls=%async_computation.2 | async-start | bytes 4063232 | tf_op jit(solution)/shard_map/all_to_all | solution.py:88
  66.9 33.7 %copy-start.16 = (u32[32]{0:T(128)S(1)}, u32[32]{0:T(128)}, u32[]{:S(2)}) copy-start(u32[32]{0:T(128)} %constant.117) | copy-start | bytes 388
  66.9 215.9 %copy-start.12 = (f32[7,3,512]{2,0,1:T(8,128)S(1)}, f32[7,3,512]{2,0,1:T(8,128)}, u32[]{:S(2)}) copy-start(f32[7,3,512]{2,0,1:T(8,128)} %param.11) | copy-start | bytes 129028
  66.9 216.0 %copy-start.14 = (f32[16,32]{1,0:T(8,128)S(1)}, f32[16,32]{1,0:T(8,128)}, u32[]{:S(2)}) copy-start(f32[16,32]{1,0:T(8,128)} %param.13) | copy-start | bytes 6148
  66.9 216.1 %copy-start.13 = (f32[16,32]{1,0:T(8,128)S(1)}, f32[16,32]{1,0:T(8,128)}, u32[]{:S(2)}) copy-start(f32[16,32]{1,0:T(8,128)} %param.12) | copy-start | bytes 6148
  94.9 271.8 %all-to-all-start = ((bf16[248,3,4096]{0,1,2:T(4,128)(2,1)}), bf16[248,3,4096]{0,1,2:T(4,128)(2,1)}, u32[]{:S(2)}, u32[]{:S(2)}) async-start(bf16[248,3,4096]{0,1,2:T(4,128)(2,1)} %copy.193), calls=%async_computation | async-start | bytes 16777216 | tf_op jit(solution)/shard_map/all_to_all | solution.py:88
  364.9 60.9 %copy-start.6 = (bf16[1024,512]{1,0:T(8,128)(2,1)}, bf16[1024,512]{1,0:T(8,128)(2,1)S(1)}, u32[]{:S(2)}) copy-start(bf16[1024,512]{1,0:T(8,128)(2,1)S(1)} %gather_fusion.3) | copy-start | bytes 3145732
  420.0 5.8 copy-start.3
  425.8 1.7 copy-start
  427.4 1.6 copy-start.8
  430.5 28.0 %copy-start.7 = (bf16[64,8,8,128]{3,2,1,0:T(8,128)(2,1)}, bf16[64,8,8,128]{3,2,1,0:T(8,128)(2,1)S(1)}, u32[]{:S(2)}) copy-start(bf16[64,8,8,128]{3,2,1,0:T(8,128)(2,1)S(1)} %copy.250) | copy-start | bytes 3145732
  438.9 2.2 copy-start.10
  446.0 4.4 copy-start.5
  446.0 4.4 copy-start.11
  450.7 121.1 %copy-start.1 = (f32[8,128,32,16]{1,0,3,2:T(8,128)}, f32[8,128,32,16]{1,0,3,2:T(8,128)S(1)}, u32[]{:S(2)}) copy-start(f32[8,128,32,16]{1,0,3,2:T(8,128)S(1)} %convert_multiply_fusion.20) | copy-start | bytes 6291460
  450.7 3.9 copy-start.4
  472.6 5.7 copy-start.9
  487.7 2.9 copy-start.15
  520.1 84.4 %all-to-all-start.1 = ((bf16[8,2,63488]{2,1,0:T(2,128)(2,1)}), bf16[8,2,63488]{2,1,0:T(2,128)(2,1)}, u32[]{:S(2)}, u32[]{:S(2)}) async-start(bf16[8,2,63488]{2,1,0:T(2,128)(2,1)} %reshape.457), calls=%async_computation.1 | async-start | bytes 4063232 | tf_op jit(solution)/shard_map/all_to_all | solution.py:93
  588.3 4.3 copy-start.2
  604.5 182.5 %all-to-all-start.3 = ((bf16[1984,3,512]{2,1,0:T(4,128)(2,1)}), bf16[1984,3,512]{2,1,0:T(4,128)(2,1)}, u32[]{:S(2)}, u32[]{:S(2)}) async-start(bf16[1984,3,512]{2,1,0:T(4,128)(2,1)} %select_select_fusion), calls=%async_computation.3 | async-start | bytes 16252928 | tf_op jit(solution)/shard_map/all_to_all | solution.py:93
where the time goes:
time: 816 us; the launch traced here: 810 us
  local copies, waits for them, and re-layouts  281 us (34%)
  blocking collectives  193 us (24%)
  waiting for transfers between devices  167 us (20%)
  other arithmetic  91 us (11%)
  matrix products  52 us (6%)
  starting transfers between devices  22.5 us (3%)
    lt x1, blocking collectives, moved_operator(): back_valid = (slot_ids[None, :] < all_counts[:, None]).reshape(-1)  181 us
    all_to_all x2, waiting for transfers between devices, outbound(): lax.all_to_all(picked, 'ctx', split_axis=0, concat_axis=2, tiled=True)  139 us
    gather x2, local copies, waits for them, and re-layouts, modal_local(): jnp.take(kernel_rows, jnp.clip(lag_grid, 0, row_block - 1), axis=1)  60.9 us
    unnamed x60, local copies, waits for them, and re-layouts  50.1 us
    all_to_all x4, local copies, waits for them, and re-layouts, inbound(): lax.all_to_all(loader_rows, 'ctx', split_axis=2, concat_axis=0, tiled=True)  40.9 us
    gather x2, local copies, waits for them, and re-layouts, outbound(): picked = jnp.take(chan_rows, back_index, axis=0)  32.7 us
    all_to_all x2, waiting for transfers between devices, inbound(): lax.all_to_all(loader_rows, 'ctx', split_axis=2, concat_axis=0, tiled=True)  27.9 us
    unnamed x1, other arithmetic  23.6 us
  transfers between devices with their start and end apart: 4, of which 2 were waited for; matrix products, arithmetic and copies ran while one was open for 26% of the time, Pallas kernels for 0%

commit v1 on v0

--- a/solution.py
+++ b/solution.py
@@ -5,6 +5,14 @@
 
 TAPS = 7
 TOK_DEV = 128
+
+
+def open_zone(message, axis_tag, dim_no, k_dim):
+    far_arr = lax.axis_size(axis_tag)
+    r_now = jnp.split(message, far_arr, axis=dim_no)
+    near = jnp.stack(r_now)
+    item_now = lax.all_to_all(near, axis_name=axis_tag, split_axis=0, concat_axis=0)
+    return jnp.concatenate(item_now, axis=k_dim)
 
 
 def modal_local(mixed, d_long, residue, decay_rate, row_block):
@@ -85,7 +93,7 @@
         return jnp.take(received, take_index, axis=0)
 
     def inbound(loader_rows):
-        return place(lax.all_to_all(loader_rows, "ctx", split_axis=2, concat_axis=0, tiled=True))
+        return place(open_zone(loader_rows, "ctx", 2, 0))
 
     def outbound(chan_rows):
         picked = jnp.take(chan_rows, back_index, axis=0)

time: 816 us -> 715 us (0.88)
  blocking collectives: 193 us -> 144 us
  local copies, waits for them, and re-layouts: 281 us -> 240 us
  waiting for transfers between devices: 167 us -> 156 us
    lt x1, blocking collectives: 181 us -> 131 us  [moved_operator(): back_valid = (slot_ids[None, :] < all_counts[:, None]).reshape(-1)]
    all_to_all x4 -> x1, local copies, waits for them, and re-layouts: 40.9 us -> 10 us  [open_zone(): lax.all_to_all(near, axis_name=axis_tag, split_axis=0, concat_axis=0)]
    unnamed x1 -> x0, other arithmetic: 23.6 us -> none
    convert_element_type x1, other arithmetic: 5.23 us -> 20.7 us  [moved_operator(): grad_rows = outbound(d_window.astype(jnp.bfloat16))]
    all_to_all x2, waiting for transfers between devices: 27.9 us -> 17.2 us  [open_zone(): lax.all_to_all(near, axis_name=axis_tag, split_axis=0, concat_axis=0)]
    another operation x2 -> x3, local copies, waits for them, and re-layouts: 20.4 us -> 10.2 us  [open_zone(): near = jnp.stack(r_now)]
    unnamed x60 -> x74, local copies, waits for them, and re-layouts: 50.1 us -> 50.8 us
  transfers between devices with their start and end apart: 4 -> 4, of which waited for: 2 -> 2; matrix products, arithmetic and copies ran while one was open for 26% -> 31% of each run, Pallas kernels for 0% -> 0%
where the time goes in v1:
time: 715 us; the launch traced here: 703 us
  local copies, waits for them, and re-layouts  240 us (34%)
  waiting for transfers between devices  156 us (22%)
  blocking collectives  144 us (20%)
  other arithmetic  88.1 us (12%)
  matrix products  49.9 us (7%)
  starting transfers between devices  22.7 us (3%)
    all_to_all x2, waiting for transfers between devices, outbound(): lax.all_to_all(picked, 'ctx', split_axis=0, concat_axis=2, tiled=True)  139 us
    lt x1, blocking collectives, moved_operator(): back_valid = (slot_ids[None, :] < all_counts[:, None]).reshape(-1)  131 us
    gather x2, local copies, waits for them, and re-layouts, modal_local(): jnp.take(kernel_rows, jnp.clip(lag_grid, 0, row_block - 1), axis=1)  60.9 us
    unnamed x74, local copies, waits for them, and re-layouts  50.8 us
    gather x2, local copies, waits for them, and re-layouts, outbound(): picked = jnp.take(chan_rows, back_index, axis=0)  32.4 us
    convert_element_type x1, other arithmetic, moved_operator(): grad_rows = outbound(d_window.astype(jnp.bfloat16))  20.7 us
    select_n x3, other arithmetic, outbound(): jnp.where(back_valid[:, None, None], picked, jnp.zeros_like(picked))  19.9 us
    gather x3, local copies, waits for them, and re-layouts, place(): return jnp.take(received, take_index, axis=0)  18.5 us
  transfers between devices with their start and end apart: 4, of which 2 were waited for; matrix products, arithmetic and copies ran while one was open for 31% of the time, Pallas kernels for 0%

profile of v1, /device:TPU:0, one launch (start us, length us, event | category | flops | bytes accessed | tf_op | source)
XLA Modules:
  0.0 703.1 jit_solution(7121414075707911399)
XLA Ops:
  10.3 7.3 %all-to-all-start.2 = ((bf16[8,248,1,512]{3,1,2,0:T(8,128)(2,1)}), bf16[8,248,1,512]{3,1,2,0:T(8,128)(2,1)S(1)}, u32[]{:S(2)}, u32[]{:S(2)}) async-start(bf16[8,248,1,512]{3,1,2,0:T(8,128)(2,1)} %fusion.86), calls=%async_computation.2 | async-start | bytes 4063232 | tf_op jit(solution)/shard_map/all_to_all | solution.py:14
  17.5 8.6 %copy.169 = bf16[1,1,248,12288]{2,3,1,0:T(8,128)(2,1)} copy(bf16[1,1,248,12288]{3,2,1,0:T(8,128)(2,1)} %param.9) | data formatting | bytes 12189696 | tf_op args[0]
  38.6 8.6 %copy.170 = bf16[8,248,3,512]{3,1,2,0:T(8,128)(2,1)} copy(bf16[8,248,3,512]{1,3,2,0:T(8,128)(2,1)} %fusion.70) | data formatting | bytes 12189696 | tf_op jit(solution)/shard_map/stack | solution.py:13
  47.2 17.2 %all-to-all-done.2 = bf16[8,248,1,512]{3,1,2,0:T(8,128)(2,1)S(1)} async-done(((bf16[8,248,1,512]{3,1,2,0:T(8,128)(2,1)}), bf16[8,248,1,512]{3,1,2,0:T(8,128)(2,1)S(1)}, u32[]{:S(2)}, u32[]{:S(2)}) %all-to-all-start.2) | async-done | bytes 2031648 | tf_op jit(solution)/shard_map/all_to_all | solution.py:14
  64.4 4.8 all-to-all-start
  71.1 131.3 %all-reduce.2 = s32[8]{0:T(128)S(1)} all-reduce(s32[8]{0:T(128)S(1)} %bitcast_dynamic-update-slice_fusion), channel_id=1, replica_groups=mesh['dp'=4,'ctx'=8] {'ctx'}, use_global_device_ids=true, to_apply=%add.2 | all-reduce | flops 8 | bytes 64 | tf_op jit(solution)/shard_map/lt | solution.py:90
  203.4 54.4 %gather_fusion.1 = f32[16384,32]{1,0:T(8,128)} fusion(f32[32,128]{0,1:T(8,128)S(1)} %copy.176, s32[16384]{0:T(1024)S(1)} %fusion.107), kind=kCustom, calls=%fused_computation.1 | custom fusion | bytes 4259840 | tf_op jit(solution)/shard_map/jit(_take)/gather | solution.py:32
  257.8 6.5 copy.177
  264.8 4.0 gather_fusion.3
  270.6 10.0 %copy.171 = bf16[8,248,3,512]{3,2,1,0:T(4,128)(2,1)} copy(bf16[8,248,3,512]{3,1,2,0:T(8,128)(2,1)} %all-to-all-done) | data formatting | bytes 12189696 | tf_op jit(solution)/shard_map/all_to_all | solution.py:14
  280.7 14.0 %gather_fusion = bf16[1024,3,512]{2,1,0:T(4,128)(2,1)} fusion(bf16[1984,3,512]{2,1,0:T(4,128)(2,1)} %bitcast.258, s32[1024]{0:T(1024)S(1)} %broadcast_clamp_fusion), kind=kCustom, calls=%fused_computation | custom fusion | bytes 6295552 | tf_op jit(solution)/shard_map/jit(_take)/gather | solution.py:93
  294.7 3.1 copy_select_fusion
  297.8 5.8 fusion.11
  306.6 2.3 copy.187
  313.0 2.8 copy.179
  317.9 3.4 fusion.45
  321.4 3.7 copy.190
  325.1 7.7 %fusion.35 = f32[16,32,16,8]{2,3,1,0:T(8,128)} fusion(f32[8,16,32,16]{3,0,2,1:T(8,128)} %copy.179, f32[8,8]{0,1:T(8,128)S(1)} %fusion.112, f32[16,32]{1,0:T(8,128)S(1)} %get-tuple-element.118, pred[8,8]{0,1:T(8,128)(4,1)S(1)} %fusion.113), kind=kOutput, calls=%fused_computation.75 | convolution fusion | flops 6356992 | bytes 526656 | tf_op jit(solution)/shard_map/rgij,jrgq->irgq/dot_general | solution.py:49
  332.8 3.9 fusion.42
  336.8 2.5 fusion.26
  339.3 4.4 add_bitcast_fusion
  345.9 2.9 reshape.396
  348.8 2.9 copy.193
  351.7 6.1 fusion.32
  357.8 2.4 add_bitcast_fusion.1
  362.4 2.7 reshape.393
  365.1 2.9 copy.183
  368.0 6.1 convert_multiply_fusion.15
  374.1 9.2 %gather_fusion.2 = bf16[1984,512]{1,0:T(8,128)(2,1)} fusion(bf16[1024,512]{1,0:T(8,128)(2,1)S(1)} %get-tuple-element.108, s32[2048]{0:T(1024)S(1)} %pad_clamp_fusion), kind=kCustom, calls=%fused_computation.2 | custom fusion | bytes 4071168 | tf_op jit(solution)/shard_map/jit(_take)/gather | solution.py:99
  383.3 3.6 fusion.36
  387.4 4.4 reduce.2
  391.8 5.9 reshape.464
  397.8 4.7 all-to-all-start.1
  402.5 16.1 %fusion.18 = (f32[3,512]{1,0:T(4,128)S(1)}, f32[3,512]{1,0:T(4,128)S(1)}, f32[3,512]{1,0:T(4,128)S(1)}, f32[3,512]{1,0:T(4,128)S(1)}, f32[3,512]{1,0:T(4,128)S(1...) fusion(bf16[1024,3,512]{2,0,1:T(8,128)(2,1)} %copy-done.3, ...), kind=kLoop, calls=%fused_computation.40 | loop fusion | flops 36165120 | bytes 15771648 | tf_op jit(solution)/shard_map/reduce_sum | solution.py:131
  418.6 14.8 %fusion.25 = f32[16,32]{0,1:T(8,128)S(1)} fusion(f32[16,32,8,16]{3,2,1,0:T(8,128)S(1)} %bitcast.257, f32[8,128,32,16]{1,0,3,2:T(8,128)S(1)} %convert_multiply_fusion.20, f32[128]{0:T(128)S(1)} %iota_add_fusion, f32[16,32]{0,1:T(8,128)S(1)} %copy.175), kind=kOutput, calls=%fused_computation.59 | convolution fusion | flops 100859392 | bytes 2363904 | tf_op jit(solution)/shard_map/iagq,rga,irgq->rg/dot_general | solution.py:66
  433.5 20.7 %add_convert_fusion = bf16[1024,3,512]{2,0,1:T(8,128)(2,1)S(1)} fusion(f32[1024,3,512]{2,0,1:T(8,128)} %get-tuple-element.106, f32[3,512]{1,0:T(4,128)S(1)} %get-tuple-element.120, f32[3,512]{1,0:T(4,128)S(1)} %get-tuple-element.121, f32[3,512]{1,0:T(4,128)S(1)} %get-tuple-element.122, f32[3,512]{1,0:T(4,128)S(1)} %get-tuple-element.123, ...), kind=kLoop, calls=%fused_computation.42 | loop fusion | flops 22020096 | bytes 9480192 | tf_op jit(solution)/shard_map/convert_element_type | solution.py:132
  454.2 4.7 copy.194
  458.9 23.3 %gather_fusion.4 = bf16[1984,3,512]{2,1,0:T(4,128)(2,1)} fusion(bf16[1024,3,512]{2,1,0:T(4,128)(2,1)} %copy.194, s32[2048]{0:T(1024)S(1)} %pad_clamp_fusion), kind=kCustom, calls=%fused_computation.4 | custom fusion | bytes 12197632 | tf_op jit(solution)/shard_map/jit(_take)/gather | solution.py:99
  482.1 3.5 convolution_bitcast_fusion
  486.1 11.9 %select_select_fusion = bf16[1984,3,512]{2,1,0:T(4,128)(2,1)} fusion(bf16[1984,3,512]{2,1,0:T(4,128)(2,1)S(1)} %copy-done.2, pred[1984]{0:T(1024)(128)(4,1)S(1)} %compare_and_fusion, pred[1984]{0:T(1024)(128)(4,1)S(1)} %lt.99), kind=kLoop, calls=%fused_computation.12 | loop fusion | flops 6094848 | bytes 12193664 | tf_op jit(solution)/shard_map/jit(_where)/select_n | solution.py:100
  498.0 6.0 all-to-all-start.3
  503.9 11.9 %while.11 = (s32[]{:T(128)}, f32[16,32]{1,0:T(8,128)S(1)}, f32[16,32]{1,0:T(8,128)S(1)}, f32[32,128,128]{2,1,0:T(8,128)S(1)}, s32[]{:T(128)}, /*index=5*/s32[]{:T(128)}) while((s32[]{:T(128)}, f32[16,32]{1,0:T(8,128)S(1)}, f32[16,32]{1,0:T(8,128)S(1)}, f32[32,128,128]{2,1,0:T(8,128)S(1)}, s32[]{:T(128)}, ...), condition=%wide.region_14.15_spmd.clone, body=%wide.region_12.14_spmd.clone.sunk | while | flops 2179074 | bytes 2261837 | solution.py:65
  515.9 12.5 %all-reduce.3 = (f32[7,3,512]{2,1,0:T(4,128)S(1)}, f32[16,32]{1,0:T(8,128)}, f32[512]{0:T(512)}) all-reduce(f32[7,3,512]{2,1,0:T(4,128)S(1)} %constant_dynamic-update-slice_fusion, f32[16,32]{1,0:T(8,128)S(1)} %add.246, f32[512]{0:T(512)S(1)} %get-tuple-element.99), channel_id=1, replica_groups=mesh['dp'=4,'ctx'=8] {'dp'}, use_global_device_ids=true, to_apply=%region_11.12 | all-reduce | flops 11776 | bytes 94208 | tf_op jit(solution)/shard_map/psum | solution.py:146
  529.0 6.8 reshape.465
  535.8 2.7 copy.217
  541.4 139.1 %all-to-all-done.3 = bf16[1984,3,512]{2,1,0:T(4,128)(2,1)} async-done(((bf16[1984,3,512]{2,1,0:T(4,128)(2,1)}), bf16[1984,3,512]{2,1,0:T(4,128)(2,1)}, u32[]{:S(2)}, u32[]{:S(2)}) %all-to-all-start.3) | async-done | bytes 6094880 | tf_op jit(solution)/shard_map/all_to_all | solution.py:101
  680.5 12.5 %copy.195 = bf16[248,3,8,512]{3,2,1,0:T(8,128)(2,1)} copy(bf16[248,3,8,512]{3,1,0,2:T(4,128)(2,1)} %bitcast.55) | data formatting | bytes 12189696 | tf_op jit(solution)/shard_map/all_to_all | solution.py:101
  693.0 9.8 %reshape.397 = bf16[1,1,248,12288]{3,2,1,0:T(8,128)(2,1)} reshape(bf16[248,3,8,512]{3,2,1,0:T(8,128)(2,1)} %copy.195) | data formatting | bytes 12189696 | tf_op jit(solution)/shard_map/reshape | solution.py:135
  (197 shorter events, 56.3 us)
Async XLA Ops:
  0.6 6.8 copy-start.13
  10.3 54.1 %all-to-all-start.2 = ((bf16[8,248,1,512]{3,1,2,0:T(8,128)(2,1)}), bf16[8,248,1,512]{3,1,2,0:T(8,128)(2,1)S(1)}, u32[]{:S(2)}, u32[]{:S(2)}) async-start(bf16[8,248,1,512]{3,1,2,0:T(8,128)(2,1)} %fusion.86), calls=%async_computation.2 | async-start | bytes 4063232 | tf_op jit(solution)/shard_map/all_to_all | solution.py:14
  26.1 8.7 %copy-start.4 = (bf16[1,1,248,12288]{2,3,1,0:T(8,128)(2,1)S(1)}, bf16[1,1,248,12288]{2,3,1,0:T(8,128)(2,1)}, u32[]{:S(2)}) copy-start(bf16[1,1,248,12288]{2,3,1,0:T(8,128)(2,1)} %copy.169) | copy-start | bytes 18284548
  47.2 22.6 %copy-start.18 = (u32[32]{0:T(128)S(1)}, u32[32]{0:T(128)}, u32[]{:S(2)}) copy-start(u32[32]{0:T(128)} %constant.117) | copy-start | bytes 388
  47.2 155.6 %copy-start.14 = (f32[7,3,512]{2,0,1:T(8,128)S(1)}, f32[7,3,512]{2,0,1:T(8,128)}, u32[]{:S(2)}) copy-start(f32[7,3,512]{2,0,1:T(8,128)} %param.11) | copy-start | bytes 129028
  47.2 155.7 %copy-start.16 = (f32[16,32]{1,0:T(8,128)S(1)}, f32[16,32]{1,0:T(8,128)}, u32[]{:S(2)}) copy-start(f32[16,32]{1,0:T(8,128)} %param.13) | copy-start | bytes 6148
  47.2 155.8 %copy-start.15 = (f32[16,32]{1,0:T(8,128)S(1)}, f32[16,32]{1,0:T(8,128)}, u32[]{:S(2)}) copy-start(f32[16,32]{1,0:T(8,128)} %param.12) | copy-start | bytes 6148
  64.4 206.3 %all-to-all-start = ((bf16[8,248,3,512]{3,1,2,0:T(8,128)(2,1)}), bf16[8,248,3,512]{3,1,2,0:T(8,128)(2,1)}, u32[]{:S(2)}, u32[]{:S(2)}) async-start(bf16[8,248,3,512]{3,1,2,0:T(8,128)(2,1)} %copy.170), calls=%async_computation | async-start | bytes 12189696 | tf_op jit(solution)/shard_map/all_to_all | solution.py:14
  268.8 36.6 %copy-start.8 = (bf16[1024,512]{1,0:T(8,128)(2,1)}, bf16[1024,512]{1,0:T(8,128)(2,1)S(1)}, u32[]{:S(2)}) copy-start(bf16[1024,512]{1,0:T(8,128)(2,1)S(1)} %gather_fusion.3) | copy-start | bytes 3145732
  297.8 5.8 copy-start.3
  303.6 2.4 copy-start
  306.6 4.1 copy-start.11
  312.0 45.8 %copy-start.9 = (bf16[64,8,8,128]{3,2,1,0:T(8,128)(2,1)}, bf16[64,8,8,128]{3,2,1,0:T(8,128)(2,1)S(1)}, u32[]{:S(2)}) copy-start(bf16[64,8,8,128]{3,2,1,0:T(8,128)(2,1)S(1)} %copy.218) | copy-start | bytes 3145732
  317.9 100.6 %copy-start.1 = (f32[8,128,32,16]{1,0,3,2:T(8,128)}, f32[8,128,32,16]{1,0,3,2:T(8,128)S(1)}, u32[]{:S(2)}) copy-start(f32[8,128,32,16]{1,0,3,2:T(8,128)S(1)} %convert_multiply_fusion.20) | copy-start | bytes 6291460
  325.1 7.7 %copy-start.12 = (f32[8,16,32,16]{3,0,2,1:T(8,128)S(1)}, f32[8,16,32,16]{3,0,2,1:T(8,128)}, u32[]{:S(2)}) copy-start(f32[8,16,32,16]{3,0,2,1:T(8,128)} %copy.190) | copy-start | bytes 786436
  332.8 4.0 copy-start.5
  351.7 6.1 copy-start.6
  365.1 2.9 copy-start.17
  397.8 100.2 %all-to-all-start.1 = ((bf16[8,2,63488]{2,1,0:T(2,128)(2,1)}), bf16[8,2,63488]{2,1,0:T(2,128)(2,1)}, u32[]{:S(2)}, u32[]{:S(2)}) async-start(bf16[8,2,63488]{2,1,0:T(2,128)(2,1)} %reshape.464), calls=%async_computation.1 | async-start | bytes 4063232 | tf_op jit(solution)/shard_map/all_to_all | solution.py:101
  402.5 16.1 %copy-start.7 = (f32[16,32,16,8]{2,3,1,0:T(8,128)S(1)}, f32[16,32,16,8]{2,3,1,0:T(8,128)}, u32[]{:S(2)}) copy-start(f32[16,32,16,8]{2,3,1,0:T(8,128)} %fusion.35) | copy-start | bytes 786436
  458.9 23.3 %copy-start.10 = (bf16[64,8,8,128]{3,2,1,0:T(8,128)(2,1)S(1)}, bf16[64,8,8,128]{3,2,1,0:T(8,128)(2,1)}, u32[]{:S(2)}) copy-start(bf16[64,8,8,128]{3,2,1,0:T(8,128)(2,1)} %copy-done.9) | copy-start | bytes 3145732
  482.1 3.9 copy-start.2
  498.0 182.5 %all-to-all-start.3 = ((bf16[1984,3,512]{2,1,0:T(4,128)(2,1)}), bf16[1984,3,512]{2,1,0:T(4,128)(2,1)}, u32[]{:S(2)}, u32[]{:S(2)}) async-start(bf16[1984,3,512]{2,1,0:T(4,128)(2,1)} %select_select_fusion), calls=%async_computation.3 | async-start | bytes 16252928 | tf_op jit(solution)/shard_map/all_to_all | solution.py:101
